TPU v7x, 512 devices: a whole 4x8x8 slice. The times are simulated.
512 devices in a mesh: lon: 32 (over x, y), lat: 4 (over z_lo, core), lev: 4 (over z_hi).
Axes of the slice: x: 4, y: 8, z: 8 (z_hi: 4, z_lo: 2; z = z_hi * 2 + z_lo), core: 2. Of those that a mesh axis runs over, the one named last changes fastest.
Arguments:
- adjoint_field: float32 [12, 12, 128, 4096], P(None, 'lev', 'lat', 'lon'), may hold values from -6 to 6
- east_courant: float32 [12, 128, 4096], P('lev', 'lat', 'lon'), may hold values from -0.2 to 0.2
- north_courant: float32 [12, 128, 4096], P('lev', 'lat', 'lon'), may hold values from -0.2 to 0.2
- pole_courant: float32 [12, 4096], P('lev', 'lon'), may hold values from -0.2 to 0.2
- mix_fraction: float32 [12, 128, 4096], P('lev', 'lat', 'lon'), may hold values from 0.05 to 0.6
- detrain_share: float32 [12, 128, 4096], P('lev', 'lat', 'lon'), may hold values from 0.1 to 3
- sounding_owner: int32 [2, 32768, 1], P(None, ('lon', 'lat')), may hold values from 0 to 127; in each aligned block of 256 rows (0 to 255, 256 to 511, ..., all dimensions but the last counted through in order) at most 4 rows name the same one
- sounding_cell: int32 [2, 32768], P(None, ('lon', 'lat')), may hold values from 0 to 4095
- sounding_count: int32 [2, 128], P(None, ('lon', 'lat')), may hold values from 1 to 256, 20480 in all within a row
- sounding_forcing: float32 [2, 12, 32768], P(None, 'lev', ('lon', 'lat')), may hold values from -6 to 6
Outputs:
- earlier_adjoint: float32 [12, 12, 128, 4096], P(None, 'lev', 'lat', 'lon')
Inputs may be any that keep to these rules, and one draw needn't show every extreme that they name: `sounding_owner`: in each aligned block of 256 slots of one step (the slots of one device) no owner is named more than 4 times, a bound that some block reaches. `sounding_count`: each step's counts sum to 20480; at each step some device has exactly 256.
All inputs are finite; a program needn't handle non-finite values.
Results may differ from a plain program's by a relative error of at most 0.0001.
Values sent between devices are 32-bit elements; how exact they have to be, the bound alone decides.
A program may use at most 128 MiB of HBM per device.

v0:
```python
import jax
import jax.numpy as jnp
from jax import lax
from jax.sharding import PartitionSpec as P


def from_behind(value, axis, steps):
    count = lax.axis_size(axis)
    pairs = [(source, (source + steps) % count) for source in range(count)]
    return lax.ppermute(value, axis, pairs)


def from_behind_2(block, axis, distance):
    devices = range(lax.axis_size(axis))
    route = [(i - distance, i) for i in devices if i - distance in devices]
    return lax.ppermute(block, axis, route)


def extended(x, sides, width, wrap):
    for axis, dim in sides:
        size, length = (lax.axis_size(axis), x.shape[dim])
        up = [(i, (i + 1) % size) for i in range(size if wrap else size - 1)]
        down = [(j, i) for i, j in up]
        last = lax.slice_in_dim(x, length - width, length, axis=dim)
        initial = lax.slice_in_dim(x, 0, width, axis=dim)
        before = lax.ppermute(last, axis, up)
        after = lax.ppermute(initial, axis, down)
        x = jnp.concatenate([before, x, after], axis=dim)
    return x


def mix_sum(partial_sum):
    return lax.psum(partial_sum, "lev")


def on_device(
    adjoint_field,
    east_courant,
    north_courant,
    pole_courant,
    mix_fraction,
    detrain_share,
    sounding_owner,
    sounding_cell,
    sounding_count,
    sounding_forcing,
):
    lon_count = lax.axis_size("lon")
    lat_count = lax.axis_size("lat")
    lat_place = lax.axis_index("lat")
    owner_self = lax.axis_index("lon") * lat_count + lat_place
    tracers, lev_dev, lat_rows, lon_cols = adjoint_field.shape
    step_count = sounding_forcing.shape[0]
    slot_count = sounding_forcing.shape[2]
    grid_cells = lat_rows * lon_cols
    owner_count = lon_count * lat_count
    cap = 4
    live_slots = jnp.arange(slot_count, dtype=jnp.int32)[None, :] < sounding_count
    values = jnp.where(live_slots[:, None, :], sounding_forcing, 0.0)
    owner_ids = sounding_owner[:, :, 0]
    slot_iota = jnp.arange(slot_count, dtype=jnp.int32)
    earlier = slot_iota[None, :, None] < slot_iota[None, None, :]
    same_owner = owner_ids[:, :, None] == owner_ids[:, None, :]
    rank = jnp.sum(jnp.logical_and(earlier, same_owner), axis=1, dtype=jnp.int32)
    position = owner_ids * cap + rank
    bucket_iota = jnp.arange(owner_count * cap, dtype=jnp.int32)
    chosen = position[:, :, None] == bucket_iota[None, None, :]
    bucket_values = jnp.sum(jnp.where(chosen[:, None, :, :], values[:, :, :, None], 0.0), axis=2)
    bucket_cell = (
        jnp.max(jnp.where(chosen, sounding_cell[:, :, None] + 1, 0), axis=1).astype(jnp.float32)
        - 1.0
    )
    packed = jnp.concatenate([bucket_values, bucket_cell[:, None, :]], axis=1)
    packed = packed.reshape(step_count, lev_dev + 1, owner_count, cap)
    packed = jnp.transpose(packed, (2, 0, 1, 3))
    arrived = lax.all_to_all(packed, ("lon", "lat"), 0, 0, tiled=True)
    arrived = jnp.transpose(arrived, (1, 2, 0, 3)).reshape(
        step_count, lev_dev + 1, owner_count * cap
    )
    cell_iota = jnp.arange(grid_cells, dtype=jnp.int32).astype(jnp.float32)
    hit = (arrived[:, lev_dev, :, None] == cell_iota[None, None, :]).astype(jnp.float32)
    forcing_grid = jnp.einsum(
        "tke,tec->tkc", arrived[:, :lev_dev, :], hit, precision=lax.Precision.HIGHEST
    )
    forcing_grid = forcing_grid.reshape(step_count, lev_dev, lat_rows, lon_cols)
    west_column = from_behind(east_courant[:, :, -1:], "lon", 1)
    west_wind = jnp.concatenate([west_column, east_courant[:, :, :-1]], axis=2)
    south_row = from_behind_2(north_courant[:, -1:, :], "lat", 1)
    south_wind = jnp.concatenate([south_row, north_courant[:, :-1, :]], axis=1)
    pole_pair = jnp.stack([north_courant[:, -1, :], pole_courant], axis=0)
    partner_winds = from_behind(pole_pair, "lon", lon_count // 2)
    row_index = jnp.arange(lat_rows, dtype=jnp.int32)[None, :, None]
    at_top = jnp.logical_and(lat_place == lat_count - 1, row_index == lat_rows - 1)
    at_bottom = jnp.logical_and(lat_place == 0, row_index == 0)
    upwind_east = jnp.maximum(east_courant, 0.0)
    upwind_west = -jnp.minimum(west_wind, 0.0)
    upwind_north = jnp.maximum(north_courant, 0.0) + jnp.where(
        at_top, -jnp.minimum(partner_winds[0], 0.0)[:, None, :], 0.0
    )
    upwind_south = jnp.where(
        at_bottom,
        (jnp.maximum(pole_courant, 0.0) - jnp.minimum(partner_winds[1], 0.0))[:, None, :],
        -jnp.minimum(south_wind, 0.0),
    )
    total_detrain = lax.psum(jnp.sum(detrain_share, axis=0), "lev")
    adjoint = adjoint_field
    for position in range(step_count):
        step_now = step_count - 1 - position
        adjoint = adjoint + forcing_grid[step_now][None]
        partial_sum = jnp.sum(detrain_share[None] * adjoint, axis=1)
        column_sum = mix_sum(partial_sum)
        adjoint = (1.0 - mix_fraction)[None] * adjoint + mix_fraction[None] * (
            column_sum / total_detrain
        )[:, None]
        across = extended(adjoint, (("lon", 3),), 1, True)
        east_side = across[:, :, :, 2:]
        west_side = across[:, :, :, :-2]
        upright = extended(adjoint, (("lat", 2),), 1, False)
        north_side = upright[:, :, 2:, :]
        south_side = upright[:, :, :-2, :]
        edge_row = jnp.where(lat_place == 0, adjoint[:, :, :1, :], adjoint[:, :, -1:, :])
        partner_row = from_behind(edge_row, "lon", lon_count // 2)
        north_side = jnp.where(at_top, partner_row, north_side)
        south_side = jnp.where(at_bottom, partner_row, south_side)
        adjoint = (
            adjoint
            + upwind_east * (east_side - adjoint)
            + upwind_west * (west_side - adjoint)
            + upwind_north * (north_side - adjoint)
            + upwind_south * (south_side - adjoint)
        )
    return adjoint


def solution(mesh):
    return jax.shard_map(
        on_device,
        mesh=mesh,
        in_specs=(
            P(None, "lev", "lat", "lon"),
            P("lev", "lat", "lon"),
            P("lev", "lat", "lon"),
            P("lev", "lon"),
            P("lev", "lat", "lon"),
            P("lev", "lat", "lon"),
            P(None, ("lon", "lat"), None),
            P(None, ("lon", "lat")),
            P(None, ("lon", "lat")),
            P(None, "lev", ("lon", "lat")),
        ),
        out_specs=P(None, "lev", "lat", "lon"),
        check_vma=False,
    )
```

profile of v0, /device:TPU:1, one launch (start us, length us, event | category | flops | bytes accessed | tf_op | source)
XLA Modules:
  0.0 237.8 jit_solution(9995370526051326967)
XLA Ops:
  6.5 0.7 slice.102
  7.2 5.4 %collective-permute-start.6 = (f32[3,1,128]{2,0,1:T(4,128)S(1)}, f32[3,1,128]{2,0,1:T(4,128)S(1)}, u32[]{:S(2)}, u32[]{:S(2)}) collective-permute-start(f32[3,1,128]{2,0,1:T(4,128)S(1)} %copy.79), channel_id=1, source_target_pairs={{0,4},{4,8},{8,12},{1,5},{5,9},{9,13},{2,6},{6,10},{10,14},{3,7},{... | collective-permute-start | bytes 4616 | tf_op jit(solution)/shard_map/ppermute | solution.py:16
  12.6 0.7 pad_maximum_fusion.8
  13.3 4.6 %collective-permute-start.3 = (f32[2,3,128]{2,1,0:T(4,128)S(1)}, f32[2,3,128]{2,1,0:T(4,128)S(1)}, u32[]{:S(2)}, u32[]{:S(2)}) collective-permute-start(f32[2,3,128]{2,1,0:T(4,128)S(1)} %pad_maximum_fusion.8), channel_id=1, source_target_pairs={{0,256},{16,272},{32,288},{48,304},{64,320},{80,336},{96,352},{112... | collective-permute-start | bytes 9224 | tf_op jit(solution)/shard_map/ppermute | solution.py:10
  18.0 0.9 slice.98
  18.8 3.2 %collective-permute-start.1 = (f32[3,32,1]{2,1,0:T(8,128)S(1)}, f32[3,32,1]{2,1,0:T(8,128)S(1)}, u32[]{:S(2)}, u32[]{:S(2)}) collective-permute-start(f32[3,32,1]{2,1,0:T(8,128)S(1)} %slice.98), channel_id=1, source_target_pairs={{0,16},{16,32},{32,48},{48,64},{64,80},{80,96},{96,112},{112,128},... | collective-permute-start | bytes 1160 | tf_op jit(solution)/shard_map/ppermute | solution.py:10
  22.1 0.7 iota_compare_fusion.2
  22.8 0.7 broadcast_add_fusion
  23.5 0.7 copy.78
  24.2 0.7 broadcast_select_fusion.2
  25.0 0.7 fusion.45
  26.3 0.4 select_reduce_fusion
  26.7 0.4 concatenate.48
  27.2 1.2 copy.40
  28.4 8.7 %all-to-all-start = ((f32[128,2,4,4]{3,1,2,0:T(2,128)}), f32[128,2,4,4]{3,1,2,0:T(2,128)S(1)}, u32[]{:S(2)}, u32[]{:S(2)}) async-start(f32[128,2,4,4]{3,1,2,0:T(2,128)} %copy.40), calls=%async_computation | async-start | bytes 1048576 | tf_op jit(solution)/shard_map/all_to_all | solution.py:76
  37.2 21.4 %psum.22 = f32[32,128]{1,0:T(8,128)S(1)} all-reduce(f32[32,128]{1,0:T(8,128)S(1)} %reduce_sum.51), channel_id=1, replica_groups=mesh['lon'=32,'lat'=4,'lev'=4] {'lev'}, use_global_device_ids=true, to_apply=%region_6.7 | all-reduce | flops 4096 | bytes 32768 | tf_op jit(solution)/shard_map/psum | solution.py:105
  59.0 0.3 reshape.146
  59.3 4.8 %fusion = f32[2,3,4096]{2,1,0:T(4,128)S(1)} fusion(f32[4096]{0:T(1024)S(1)} %iota_convert_fusion, f32[2,512]{1,0:T(2,128)S(1)} %bitcast.56, f32[2,4,512]{2,1,0:T(4,128)S(1)} %reshape.146), kind=kOutput, calls=%fused_computation | convolution fusion | flops 155189248 | bytes 135168 | tf_op jit(solution)/shard_map/tke,tec->tkc/dot_general | solution.py:82
  64.2 1.1 fusion.36
  65.4 56.0 %all-reduce.3.cloned.1.call-done = f32[12,32,128]{2,0,1:T(8,128)} async-done(((f32[12,32,128]{2,0,1:T(8,128)}), f32[12,32,128]{2,0,1:T(8,128)}) %all-reduce.3.cloned.1.call-update) | async-done | bytes 196624 | tf_op jit(solution)/shard_map/psum | solution.py:33
  121.4 1.0 broadcast_divide_fusion.1
  122.4 0.5 fusion.35
  122.9 0.6 broadcast_select_fusion.1
  123.8 4.6 %collective-permute-start.4 = (f32[12,3,1,128]{3,0,2,1:T(8,128)}, f32[12,3,1,128]{3,0,2,1:T(8,128)}, u32[]{:S(2)}, u32[]{:S(2)}) collective-permute-start(f32[12,3,1,128]{3,0,2,1:T(8,128)} %get-tuple-element.14), channel_id=1, source_target_pairs={{0,256},{16,272},{32,288},{48,304},{64,320},{80,336},{96,352},{112... | collective-permute-start | bytes 55304 | tf_op jit(solution)/shard_map/ppermute | solution.py:10
  128.3 5.3 %collective-permute-start.7 = (f32[12,3,1,128]{3,0,2,1:T(8,128)}, f32[12,3,1,128]{3,0,2,1:T(8,128)}, u32[]{:S(2)}, u32[]{:S(2)}) collective-permute-start(f32[12,3,1,128]{3,0,2,1:T(8,128)} %get-tuple-element.15), channel_id=1, source_target_pairs={{0,4},{4,8},{8,12},{1,5},{5,9},{9,13},{2,6},{6,10},{10,14},{3,7},{... | collective-permute-start | bytes 55304 | tf_op jit(solution)/shard_map/ppermute | solution.py:26
  133.7 2.1 collective-permute-start.5
  135.8 0.3 copy.43
  136.1 0.3 copy.45
  136.4 3.1 %collective-permute-start.2 = (f32[12,3,32,1]{2,3,1,0:T(1,128)S(1)}, f32[12,3,32,1]{2,3,1,0:T(1,128)S(1)}, u32[]{:S(2)}, u32[]{:S(2)}) collective-permute-start(f32[12,3,32,1]{2,3,1,0:T(1,128)S(1)} %copy.45), channel_id=1, source_target_pairs={{0,16},{16,32},{32,48},{48,64},{64,80},{80,96},{96,112},{112,128},... | collective-permute-start | bytes 13832 | tf_op jit(solution)/shard_map/ppermute | solution.py:26
  139.6 5.5 %collective-permute-start = (f32[12,3,32,1]{2,3,1,0:T(1,128)S(1)}, f32[12,3,32,1]{2,3,1,0:T(1,128)S(1)}, u32[]{:S(2)}, u32[]{:S(2)}) collective-permute-start(f32[12,3,32,1]{2,3,1,0:T(1,128)S(1)} %copy.43), channel_id=1, source_target_pairs={{16,0},{32,16},{48,32},{64,48},{80,64},{96,80},{112,96},{128,112},... | collective-permute-start | bytes 13832 | tf_op jit(solution)/shard_map/ppermute | solution.py:27
  145.2 0.8 collective-permute-done
  145.9 0.4 copy.44
  146.3 0.4 copy.46
  146.8 2.3 multiply_reduce_fusion
  149.2 52.8 %all-reduce.5.cloned.1.call-done = f32[12,32,128]{2,0,1:T(8,128)} async-done(((f32[12,32,128]{2,0,1:T(8,128)}), f32[12,32,128]{2,0,1:T(8,128)}) %all-reduce.5.cloned.1.call-update) | async-done | bytes 196624 | tf_op jit(solution)/shard_map/psum | solution.py:33
  201.9 1.0 broadcast_divide_fusion
  203.1 4.6 %collective-permute-start.10 = (f32[12,3,1,128]{3,0,2,1:T(8,128)S(1)}, f32[12,3,1,128]{3,0,2,1:T(8,128)S(1)}, u32[]{:S(2)}, u32[]{:S(2)}) collective-permute-start(f32[12,3,1,128]{3,0,2,1:T(8,128)S(1)} %get-tuple-element.7), channel_id=1, source_target_pairs={{0,256},{16,272},{32,288},{48,304},{64,320},{80,336},{96,352},{112... | collective-permute-start | bytes 55304 | tf_op jit(solution)/shard_map/ppermute | solution.py:10
  207.6 5.3 %collective-permute-start.12 = (f32[12,3,1,128]{3,0,2,1:T(8,128)S(1)}, f32[12,3,1,128]{3,0,2,1:T(8,128)S(1)}, u32[]{:S(2)}, u32[]{:S(2)}) collective-permute-start(f32[12,3,1,128]{3,0,2,1:T(8,128)S(1)} %get-tuple-element.8), channel_id=1, source_target_pairs={{0,4},{4,8},{8,12},{1,5},{5,9},{9,13},{2,6},{6,10},{10,14},{3,7},{... | collective-permute-start | bytes 55304 | tf_op jit(solution)/shard_map/ppermute | solution.py:26
  213.0 1.9 collective-permute-start.11
  215.2 0.3 copy.49
  215.5 5.1 %collective-permute-start.8 = (f32[12,3,32,1]{2,3,1,0:T(1,128)S(1)}, f32[12,3,32,1]{2,3,1,0:T(1,128)S(1)}, u32[]{:S(2)}, u32[]{:S(2)}) collective-permute-start(f32[12,3,32,1]{2,3,1,0:T(1,128)S(1)} %copy.49), channel_id=1, source_target_pairs={{16,0},{32,16},{48,32},{64,48},{80,64},{96,80},{112,96},{128,112},... | collective-permute-start | bytes 13832 | tf_op jit(solution)/shard_map/ppermute | solution.py:27
  220.6 0.3 copy.51
  220.9 1.9 collective-permute-start.9
  222.8 0.4 copy.50
  223.3 5.5 %collective-permute-done.9 = f32[12,3,32,1]{2,3,1,0:T(1,128)S(1)} collective-permute-done((f32[12,3,32,1]{2,3,1,0:T(1,128)S(1)}, f32[12,3,32,1]{2,3,1,0:T(1,128)S(1)}, u32[]{:S(2)}, u32[]{:S(2)}) %collective-permute-start.9) | collective-permute-done | bytes 4640 | tf_op jit(solution)/shard_map/ppermute | solution.py:26
  228.7 0.4 copy.52
  229.2 0.8 fusion.7
  230.0 1.0 copy.53
  (67 shorter events, 2.1 us)
Async XLA Ops:
  7.2 51.5 %collective-permute-start.6 = (f32[3,1,128]{2,0,1:T(4,128)S(1)}, f32[3,1,128]{2,0,1:T(4,128)S(1)}, u32[]{:S(2)}, u32[]{:S(2)}) collective-permute-start(f32[3,1,128]{2,0,1:T(4,128)S(1)} %copy.79), channel_id=1, source_target_pairs={{0,4},{4,8},{8,12},{1,5},{5,9},{9,13},{2,6},{6,10},{10,14},{3,7},{... | collective-permute-start | bytes 4616 | tf_op jit(solution)/shard_map/ppermute | solution.py:16
  13.3 45.5 %collective-permute-start.3 = (f32[2,3,128]{2,1,0:T(4,128)S(1)}, f32[2,3,128]{2,1,0:T(4,128)S(1)}, u32[]{:S(2)}, u32[]{:S(2)}) collective-permute-start(f32[2,3,128]{2,1,0:T(4,128)S(1)} %pad_maximum_fusion.8), channel_id=1, source_target_pairs={{0,256},{16,272},{32,288},{48,304},{64,320},{80,336},{96,352},{112... | collective-permute-start | bytes 9224 | tf_op jit(solution)/shard_map/ppermute | solution.py:10
  18.8 39.8 %collective-permute-start.1 = (f32[3,32,1]{2,1,0:T(8,128)S(1)}, f32[3,32,1]{2,1,0:T(8,128)S(1)}, u32[]{:S(2)}, u32[]{:S(2)}) collective-permute-start(f32[3,32,1]{2,1,0:T(8,128)S(1)} %slice.98), channel_id=1, source_target_pairs={{0,16},{16,32},{32,48},{48,64},{64,80},{80,96},{96,112},{112,128},... | collective-permute-start | bytes 1160 | tf_op jit(solution)/shard_map/ppermute | solution.py:10
  28.4 8.7 %copy-start.2 = (f32[3,32,128]{2,1,0:T(8,128)S(1)}, f32[3,32,128]{2,1,0:T(8,128)}, u32[]{:S(2)}) copy-start(f32[3,32,128]{2,1,0:T(8,128)} %param.11) | copy-start | bytes 147460
  28.4 8.8 %copy-start.3 = (f32[3,32,128]{2,1,0:T(8,128)S(1)}, f32[3,32,128]{2,1,0:T(8,128)}, u32[]{:S(2)}) copy-start(f32[3,32,128]{2,1,0:T(8,128)} %param.14) | copy-start | bytes 147460
  28.4 8.8 %copy-start.1 = (f32[3,32,128]{2,1,0:T(8,128)S(1)}, f32[3,32,128]{2,1,0:T(8,128)}, u32[]{:S(2)}) copy-start(f32[3,32,128]{2,1,0:T(8,128)} %param.15) | copy-start | bytes 147460
  28.4 30.4 %copy-start.4 = (f32[3,32,128]{2,1,0:T(8,128)S(1)}, f32[3,32,128]{2,1,0:T(8,128)}, u32[]{:S(2)}) copy-start(f32[3,32,128]{2,1,0:T(8,128)} %param.12) | copy-start | bytes 147460
  28.4 30.5 %all-to-all-start = ((f32[128,2,4,4]{3,1,2,0:T(2,128)}), f32[128,2,4,4]{3,1,2,0:T(2,128)S(1)}, u32[]{:S(2)}, u32[]{:S(2)}) async-start(f32[128,2,4,4]{3,1,2,0:T(2,128)} %copy.40), calls=%async_computation | async-start | bytes 1048576 | tf_op jit(solution)/shard_map/all_to_all | solution.py:76
  37.1 84.3 %all-reduce.3.cloned.1.call-start = ((), (), s32[]{:S(2)}) async-start(), calls=%async_computation.1 | async-start | bytes 524288 | tf_op jit(solution)/shard_map/psum | solution.py:33
  37.2 26.9 %copy-start.7 = (pred[32]{0:T(512)(128)(4,1)}, pred[32]{0:T(512)(128)(4,1)S(1)}, u32[]{:S(2)}) copy-start(pred[32]{0:T(512)(128)(4,1)S(1)} %get-tuple-element.22) | copy-start | bytes 100
  37.2 107.8 %copy-start.5 = (pred[32]{0:T(512)(128)(4,1)}, pred[32]{0:T(512)(128)(4,1)S(1)}, u32[]{:S(2)}) copy-start(pred[32]{0:T(512)(128)(4,1)S(1)} %get-tuple-element.21) | copy-start | bytes 100
  59.3 4.8 %copy-start = (f32[12,3,32,128]{3,2,1,0:T(8,128)S(1)}, f32[12,3,32,128]{3,2,1,0:T(8,128)}, u32[]{:S(2)}) copy-start(f32[12,3,32,128]{3,2,1,0:T(8,128)} %param.10) | copy-start | bytes 1769476
  64.1 1.2 copy-start.9
  65.3 136.6 %all-reduce.5.cloned.1.call-start = ((), (), s32[]{:S(2)}) async-start(), calls=%async_computation.2 | async-start | bytes 524288 | tf_op jit(solution)/shard_map/psum | solution.py:33
  123.8 23.0 %collective-permute-start.4 = (f32[12,3,1,128]{3,0,2,1:T(8,128)}, f32[12,3,1,128]{3,0,2,1:T(8,128)}, u32[]{:S(2)}, u32[]{:S(2)}) collective-permute-start(f32[12,3,1,128]{3,0,2,1:T(8,128)} %get-tuple-element.14), channel_id=1, source_target_pairs={{0,256},{16,272},{32,288},{48,304},{64,320},{80,336},{96,352},{112... | collective-permute-start | bytes 55304 | tf_op jit(solution)/shard_map/ppermute | solution.py:10
  128.3 18.4 %collective-permute-start.7 = (f32[12,3,1,128]{3,0,2,1:T(8,128)}, f32[12,3,1,128]{3,0,2,1:T(8,128)}, u32[]{:S(2)}, u32[]{:S(2)}) collective-permute-start(f32[12,3,1,128]{3,0,2,1:T(8,128)} %get-tuple-element.15), channel_id=1, source_target_pairs={{0,4},{4,8},{8,12},{1,5},{5,9},{9,13},{2,6},{6,10},{10,14},{3,7},{... | collective-permute-start | bytes 55304 | tf_op jit(solution)/shard_map/ppermute | solution.py:26
  133.7 13.1 %collective-permute-start.5 = (f32[12,3,1,128]{3,0,2,1:T(8,128)}, f32[12,3,1,128]{3,0,2,1:T(8,128)}, u32[]{:S(2)}, u32[]{:S(2)}) collective-permute-start(f32[12,3,1,128]{3,0,2,1:T(8,128)} %get-tuple-element.16), channel_id=1, source_target_pairs={{4,0},{8,4},{12,8},{5,1},{9,5},{13,9},{6,2},{10,6},{14,10},{7,3},{... | collective-permute-start | bytes 55304 | tf_op jit(solution)/shard_map/ppermute | solution.py:27
  136.4 9.9 %collective-permute-start.2 = (f32[12,3,32,1]{2,3,1,0:T(1,128)S(1)}, f32[12,3,32,1]{2,3,1,0:T(1,128)S(1)}, u32[]{:S(2)}, u32[]{:S(2)}) collective-permute-start(f32[12,3,32,1]{2,3,1,0:T(1,128)S(1)} %copy.45), channel_id=1, source_target_pairs={{0,16},{16,32},{32,48},{48,64},{64,80},{80,96},{96,112},{112,128},... | collective-permute-start | bytes 13832 | tf_op jit(solution)/shard_map/ppermute | solution.py:26
  139.6 6.4 %collective-permute-start = (f32[12,3,32,1]{2,3,1,0:T(1,128)S(1)}, f32[12,3,32,1]{2,3,1,0:T(1,128)S(1)}, u32[]{:S(2)}, u32[]{:S(2)}) collective-permute-start(f32[12,3,32,1]{2,3,1,0:T(1,128)S(1)} %copy.43), channel_id=1, source_target_pairs={{16,0},{32,16},{48,32},{64,48},{80,64},{96,80},{112,96},{128,112},... | collective-permute-start | bytes 13832 | tf_op jit(solution)/shard_map/ppermute | solution.py:27
  203.1 26.1 %collective-permute-start.10 = (f32[12,3,1,128]{3,0,2,1:T(8,128)S(1)}, f32[12,3,1,128]{3,0,2,1:T(8,128)S(1)}, u32[]{:S(2)}, u32[]{:S(2)}) collective-permute-start(f32[12,3,1,128]{3,0,2,1:T(8,128)S(1)} %get-tuple-element.7), channel_id=1, source_target_pairs={{0,256},{16,272},{32,288},{48,304},{64,320},{80,336},{96,352},{112... | collective-permute-start | bytes 55304 | tf_op jit(solution)/shard_map/ppermute | solution.py:10
  207.6 21.5 %collective-permute-start.12 = (f32[12,3,1,128]{3,0,2,1:T(8,128)S(1)}, f32[12,3,1,128]{3,0,2,1:T(8,128)S(1)}, u32[]{:S(2)}, u32[]{:S(2)}) collective-permute-start(f32[12,3,1,128]{3,0,2,1:T(8,128)S(1)} %get-tuple-element.8), channel_id=1, source_target_pairs={{0,4},{4,8},{8,12},{1,5},{5,9},{9,13},{2,6},{6,10},{10,14},{3,7},{... | collective-permute-start | bytes 55304 | tf_op jit(solution)/shard_map/ppermute | solution.py:26
  213.0 16.2 %collective-permute-start.11 = (f32[12,3,1,128]{3,0,2,1:T(8,128)S(1)}, f32[12,3,1,128]{3,0,2,1:T(8,128)S(1)}, u32[]{:S(2)}, u32[]{:S(2)}) collective-permute-start(f32[12,3,1,128]{3,0,2,1:T(8,128)S(1)} %get-tuple-element.9), channel_id=1, source_target_pairs={{4,0},{8,4},{12,8},{5,1},{9,5},{13,9},{6,2},{10,6},{14,10},{7,3},{... | collective-permute-start | bytes 55304 | tf_op jit(solution)/shard_map/ppermute | solution.py:27
  215.5 7.3 %collective-permute-start.8 = (f32[12,3,32,1]{2,3,1,0:T(1,128)S(1)}, f32[12,3,32,1]{2,3,1,0:T(1,128)S(1)}, u32[]{:S(2)}, u32[]{:S(2)}) collective-permute-start(f32[12,3,32,1]{2,3,1,0:T(1,128)S(1)} %copy.49), channel_id=1, source_target_pairs={{16,0},{32,16},{48,32},{64,48},{80,64},{96,80},{112,96},{128,112},... | collective-permute-start | bytes 13832 | tf_op jit(solution)/shard_map/ppermute | solution.py:27
  220.9 8.3 %copy-start.6 = (pred[32]{0:T(512)(128)(4,1)S(1)}, pred[32]{0:T(512)(128)(4,1)}, u32[]{:S(2)}) copy-start(pred[32]{0:T(512)(128)(4,1)} %copy-done.5) | copy-start | bytes 100
  220.9 8.3 %copy-start.8 = (pred[32]{0:T(512)(128)(4,1)S(1)}, pred[32]{0:T(512)(128)(4,1)}, u32[]{:S(2)}) copy-start(pred[32]{0:T(512)(128)(4,1)} %copy-done.7) | copy-start | bytes 100
  220.9 7.8 %collective-permute-start.9 = (f32[12,3,32,1]{2,3,1,0:T(1,128)S(1)}, f32[12,3,32,1]{2,3,1,0:T(1,128)S(1)}, u32[]{:S(2)}, u32[]{:S(2)}) collective-permute-start(f32[12,3,32,1]{2,3,1,0:T(1,128)S(1)} %copy.51), channel_id=1, source_target_pairs={{0,16},{16,32},{32,48},{48,64},{64,80},{80,96},{96,112},{112,128},... | collective-permute-start | bytes 13832 | tf_op jit(solution)/shard_map/ppermute | solution.py:26
Sparse Core Ops, SparseCore 0:
  65.4 55.9 all-reduce.2
  149.3 52.6 all-reduce.4
where the time goes:
time: 239 us; the launch traced here: 238 us
  waiting for transfers between devices  115 us (48%)
  starting transfers between devices  61.3 us (26%)
  blocking collectives  21.4 us (9%)
  between operations  14 us (6%)
  other arithmetic  12.2 us (5%)
  local copies, waits for them, and re-layouts  9.05 us (4%)
  matrix products  4.78 us (2%)
    psum x2, waiting for transfers between devices, mix_sum(): return lax.psum(partial_sum, 'lev')  109 us
    psum x1, blocking collectives, on_device(): total_detrain = lax.psum(jnp.sum(detrain_share, axis=0), 'lev')  21.4 us
    ppermute x4, starting transfers between devices, from_behind(): return lax.ppermute(value, axis, pairs)  17 us
    ppermute x4, starting transfers between devices, extended(): before = lax.ppermute(last, axis, up)  15.6 us
    ppermute x4, starting transfers between devices, extended(): after = lax.ppermute(initial, axis, down)  14.6 us
    all_to_all x1, starting transfers between devices, on_device(): arrived = lax.all_to_all(packed, ('lon', 'lat'), 0, 0, tiled=True)  8.66 us
    ppermute x4, waiting for transfers between devices, extended(): before = lax.ppermute(last, axis, up)  5.48 us
    ppermute x1, starting transfers between devices, from_behind_2(): return lax.ppermute(block, axis, route)  5.38 us
  transfers between devices with their start and end apart: 16, of which 4 were waited for; matrix products, arithmetic and copies ran while one was open for 5% of the time, Pallas kernels for 0%

commit v1 on v0

--- a/solution.py
+++ b/solution.py
@@ -102,7 +102,9 @@
         (jnp.maximum(pole_courant, 0.0) - jnp.minimum(partner_winds[1], 0.0))[:, None, :],
         -jnp.minimum(south_wind, 0.0),
     )
-    total_detrain = lax.psum(jnp.sum(detrain_share, axis=0), "lev")
+    block_2 = jnp.sum(detrain_share, axis=0)
+    parts = lax.all_gather(block_2, "lev")
+    total_detrain = jnp.sum(parts, axis=0)
     adjoint = adjoint_field
     for position in range(step_count):
         step_now = step_count - 1 - position

time: 239 us -> 234 us (0.979)
  blocking collectives: 21.4 us -> 16.4 us
    psum x1 -> x0, blocking collectives: 21.4 us -> none  [on_device(): total_detrain = lax.psum(jnp.sum(detrain_share, axis=0), 'lev')]
    all_gather x0 -> x1, blocking collectives: none -> 16.4 us  [on_device(): parts = lax.all_gather(block_2, 'lev')]
  transfers between devices with their start and end apart: 16 -> 16, of which waited for: 4 -> 5; matrix products, arithmetic and copies ran while one was open for 5% -> 5% of each run, Pallas kernels for 0% -> 0%
where the time goes in v1:
time: 234 us; the launch traced here: 233 us
  waiting for transfers between devices  115 us (49%)
  starting transfers between devices  61.3 us (26%)
  blocking collectives  16.4 us (7%)
  between operations  14 us (6%)
  other arithmetic  12.2 us (5%)
  local copies, waits for them, and re-layouts  9.05 us (4%)
  matrix products  4.78 us (2%)
    psum x2, waiting for transfers between devices, mix_sum(): return lax.psum(partial_sum, 'lev')  107 us
    ppermute x4, starting transfers between devices, from_behind(): return lax.ppermute(value, axis, pairs)  17 us
    all_gather x1, blocking collectives, on_device(): parts = lax.all_gather(block_2, 'lev')  16.4 us
    ppermute x4, starting transfers between devices, extended(): before = lax.ppermute(last, axis, up)  15.6 us
    ppermute x4, starting transfers between devices, extended(): after = lax.ppermute(initial, axis, down)  14.6 us
    all_to_all x1, starting transfers between devices, on_device(): arrived = lax.all_to_all(packed, ('lon', 'lat'), 0, 0, tiled=True)  8.66 us
    ppermute x4, waiting for transfers between devices, extended(): before = lax.ppermute(last, axis, up)  5.48 us
    ppermute x1, starting transfers between devices, from_behind_2(): return lax.ppermute(block, axis, route)  5.38 us
  transfers between devices with their start and end apart: 16, of which 5 were waited for; matrix products, arithmetic and copies ran while one was open for 5% of the time, Pallas kernels for 0%

profile of v1, /device:TPU:1, one launch (start us, length us, event | category | flops | bytes accessed | tf_op | source)
XLA Modules:
  0.0 233.1 jit_solution(4173391218451256072)
XLA Ops:
  6.5 0.7 slice.102
  7.2 5.4 %collective-permute-start.6 = (f32[3,1,128]{2,0,1:T(4,128)S(1)}, f32[3,1,128]{2,0,1:T(4,128)S(1)}, u32[]{:S(2)}, u32[]{:S(2)}) collective-permute-start(f32[3,1,128]{2,0,1:T(4,128)S(1)} %copy.79), channel_id=1, source_target_pairs={{0,4},{4,8},{8,12},{1,5},{5,9},{9,13},{2,6},{6,10},{10,14},{3,7},{... | collective-permute-start | bytes 4616 | tf_op jit(solution)/shard_map/ppermute | solution.py:16
  12.6 0.7 pad_maximum_fusion.8
  13.3 4.6 %collective-permute-start.3 = (f32[2,3,128]{2,1,0:T(4,128)S(1)}, f32[2,3,128]{2,1,0:T(4,128)S(1)}, u32[]{:S(2)}, u32[]{:S(2)}) collective-permute-start(f32[2,3,128]{2,1,0:T(4,128)S(1)} %pad_maximum_fusion.8), channel_id=1, source_target_pairs={{0,256},{16,272},{32,288},{48,304},{64,320},{80,336},{96,352},{112... | collective-permute-start | bytes 9224 | tf_op jit(solution)/shard_map/ppermute | solution.py:10
  18.0 0.9 slice.98
  18.8 3.2 %collective-permute-start.1 = (f32[3,32,1]{2,1,0:T(8,128)S(1)}, f32[3,32,1]{2,1,0:T(8,128)S(1)}, u32[]{:S(2)}, u32[]{:S(2)}) collective-permute-start(f32[3,32,1]{2,1,0:T(8,128)S(1)} %slice.98), channel_id=1, source_target_pairs={{0,16},{16,32},{32,48},{48,64},{64,80},{80,96},{96,112},{112,128},... | collective-permute-start | bytes 1160 | tf_op jit(solution)/shard_map/ppermute | solution.py:10
  22.1 0.7 iota_compare_fusion.2
  22.8 0.7 broadcast_add_fusion
  23.5 0.7 copy.78
  24.2 0.7 broadcast_select_fusion.2
  25.0 0.7 fusion.45
  26.3 0.4 select_reduce_fusion
  26.7 0.4 concatenate.48
  27.2 1.2 copy.40
  28.4 8.7 %all-to-all-start = ((f32[128,2,4,4]{3,1,2,0:T(2,128)}), f32[128,2,4,4]{3,1,2,0:T(2,128)S(1)}, u32[]{:S(2)}, u32[]{:S(2)}) async-start(f32[128,2,4,4]{3,1,2,0:T(2,128)} %copy.40), calls=%async_computation | async-start | bytes 1048576 | tf_op jit(solution)/shard_map/all_to_all | solution.py:76
  37.2 16.4 %all-gather = f32[128,128]{1,0:T(8,128)S(1)} all-gather(f32[32,128]{1,0:T(8,128)S(1)} %reduce_sum.60), channel_id=2, replica_groups=mesh['lon'=32,'lat'=4,'lev'=4] {'lev'}, dimensions={0}, use_global_device_ids=true | all-gather | bytes 81920 | tf_op jit(solution)/shard_map/all_gather | solution.py:106
  53.9 2.1 all-to-all-done
  56.4 4.8 %fusion = f32[2,3,4096]{2,1,0:T(4,128)S(1)} fusion(f32[4096]{0:T(1024)S(1)} %iota_convert_fusion, f32[2,512]{1,0:T(2,128)S(1)} %bitcast.58, f32[2,4,512]{2,1,0:T(4,128)S(1)} %reshape.146), kind=kOutput, calls=%fused_computation | convolution fusion | flops 155189248 | bytes 135168 | tf_op jit(solution)/shard_map/tke,tec->tkc/dot_general | solution.py:82
  61.3 1.1 fusion.36
  62.5 54.4 %all-reduce.3.cloned.1.call-done = f32[12,32,128]{2,0,1:T(8,128)} async-done(((f32[12,32,128]{2,0,1:T(8,128)}), f32[12,32,128]{2,0,1:T(8,128)}) %all-reduce.3.cloned.1.call-update) | async-done | bytes 196624 | tf_op jit(solution)/shard_map/psum | solution.py:33
  116.9 1.0 broadcast_divide_fusion.1
  117.9 0.5 fusion.35
  118.3 0.6 broadcast_select_fusion.1
  119.2 4.6 %collective-permute-start.4 = (f32[12,3,1,128]{3,0,2,1:T(8,128)}, f32[12,3,1,128]{3,0,2,1:T(8,128)}, u32[]{:S(2)}, u32[]{:S(2)}) collective-permute-start(f32[12,3,1,128]{3,0,2,1:T(8,128)} %get-tuple-element.14), channel_id=1, source_target_pairs={{0,256},{16,272},{32,288},{48,304},{64,320},{80,336},{96,352},{112... | collective-permute-start | bytes 55304 | tf_op jit(solution)/shard_map/ppermute | solution.py:10
  123.8 5.3 %collective-permute-start.7 = (f32[12,3,1,128]{3,0,2,1:T(8,128)}, f32[12,3,1,128]{3,0,2,1:T(8,128)}, u32[]{:S(2)}, u32[]{:S(2)}) collective-permute-start(f32[12,3,1,128]{3,0,2,1:T(8,128)} %get-tuple-element.15), channel_id=1, source_target_pairs={{0,4},{4,8},{8,12},{1,5},{5,9},{9,13},{2,6},{6,10},{10,14},{3,7},{... | collective-permute-start | bytes 55304 | tf_op jit(solution)/shard_map/ppermute | solution.py:26
  129.1 1.9 collective-permute-start.5
  131.1 0.3 copy.43
  131.4 0.3 copy.45
  131.7 3.1 %collective-permute-start.2 = (f32[12,3,32,1]{2,3,1,0:T(1,128)S(1)}, f32[12,3,32,1]{2,3,1,0:T(1,128)S(1)}, u32[]{:S(2)}, u32[]{:S(2)}) collective-permute-start(f32[12,3,32,1]{2,3,1,0:T(1,128)S(1)} %copy.45), channel_id=1, source_target_pairs={{0,16},{16,32},{32,48},{48,64},{64,80},{80,96},{96,112},{112,128},... | collective-permute-start | bytes 13832 | tf_op jit(solution)/shard_map/ppermute | solution.py:26
  134.8 5.7 %collective-permute-start = (f32[12,3,32,1]{2,3,1,0:T(1,128)S(1)}, f32[12,3,32,1]{2,3,1,0:T(1,128)S(1)}, u32[]{:S(2)}, u32[]{:S(2)}) collective-permute-start(f32[12,3,32,1]{2,3,1,0:T(1,128)S(1)} %copy.43), channel_id=1, source_target_pairs={{16,0},{32,16},{48,32},{64,48},{80,64},{96,80},{112,96},{128,112},... | collective-permute-start | bytes 13832 | tf_op jit(solution)/shard_map/ppermute | solution.py:27
  140.6 0.6 collective-permute-done
  141.2 0.4 copy.44
  141.6 0.4 copy.46
  142.1 2.3 %multiply_reduce_fusion = (f32[12,32,128]{2,0,1:T(8,128)}, f32[12,3,32,128]{3,0,2,1:T(8,128)S(1)}) fusion(f32[3,32,128]{2,1,0:T(8,128)S(1)} %copy-done.1, f32[3,32,128]{2,1,0:T(8,128)S(1)} %bitcast.53, f32[12,3,32,128]{3,0,2,1:T(8,128)S(1)} %fusion.35, f32[12,3,1,128]{3,0,2,1:T(8,128)} %collective-permute-done.7, pred[32]{0:T(512)(128)(4,1)} %copy-done.5, ...), kind=kLoop, calls=%fused_computation.50 | loop fusion | flops 3047424 | bytes 1735744 | tf_op jit(solution)/shard_map/reduce_sum | solution.py:112
  144.5 52.8 %all-reduce.5.cloned.1.call-done = f32[12,32,128]{2,0,1:T(8,128)} async-done(((f32[12,32,128]{2,0,1:T(8,128)}), f32[12,32,128]{2,0,1:T(8,128)}) %all-reduce.5.cloned.1.call-update) | async-done | bytes 196624 | tf_op jit(solution)/shard_map/psum | solution.py:33
  197.2 1.0 broadcast_divide_fusion
  198.4 4.6 %collective-permute-start.10 = (f32[12,3,1,128]{3,0,2,1:T(8,128)S(1)}, f32[12,3,1,128]{3,0,2,1:T(8,128)S(1)}, u32[]{:S(2)}, u32[]{:S(2)}) collective-permute-start(f32[12,3,1,128]{3,0,2,1:T(8,128)S(1)} %get-tuple-element.7), channel_id=1, source_target_pairs={{0,256},{16,272},{32,288},{48,304},{64,320},{80,336},{96,352},{112... | collective-permute-start | bytes 55304 | tf_op jit(solution)/shard_map/ppermute | solution.py:10
  202.9 5.3 %collective-permute-start.12 = (f32[12,3,1,128]{3,0,2,1:T(8,128)S(1)}, f32[12,3,1,128]{3,0,2,1:T(8,128)S(1)}, u32[]{:S(2)}, u32[]{:S(2)}) collective-permute-start(f32[12,3,1,128]{3,0,2,1:T(8,128)S(1)} %get-tuple-element.8), channel_id=1, source_target_pairs={{0,4},{4,8},{8,12},{1,5},{5,9},{9,13},{2,6},{6,10},{10,14},{3,7},{... | collective-permute-start | bytes 55304 | tf_op jit(solution)/shard_map/ppermute | solution.py:26
  208.2 1.9 collective-permute-start.11
  210.4 0.3 copy.49
  210.8 5.1 %collective-permute-start.8 = (f32[12,3,32,1]{2,3,1,0:T(1,128)S(1)}, f32[12,3,32,1]{2,3,1,0:T(1,128)S(1)}, u32[]{:S(2)}, u32[]{:S(2)}) collective-permute-start(f32[12,3,32,1]{2,3,1,0:T(1,128)S(1)} %copy.49), channel_id=1, source_target_pairs={{16,0},{32,16},{48,32},{64,48},{80,64},{96,80},{112,96},{128,112},... | collective-permute-start | bytes 13832 | tf_op jit(solution)/shard_map/ppermute | solution.py:27
  215.8 0.3 copy.51
  216.2 1.9 collective-permute-start.9
  218.1 0.4 copy.50
  218.5 5.5 %collective-permute-done.9 = f32[12,3,32,1]{2,3,1,0:T(1,128)S(1)} collective-permute-done((f32[12,3,32,1]{2,3,1,0:T(1,128)S(1)}, f32[12,3,32,1]{2,3,1,0:T(1,128)S(1)}, u32[]{:S(2)}, u32[]{:S(2)}) %collective-permute-start.9) | collective-permute-done | bytes 4640 | tf_op jit(solution)/shard_map/ppermute | solution.py:26
  224.0 0.4 copy.52
  224.5 0.8 fusion.7
  225.2 1.0 copy.53
  (68 shorter events, 2.4 us)
Async XLA Ops:
  7.2 46.5 %collective-permute-start.6 = (f32[3,1,128]{2,0,1:T(4,128)S(1)}, f32[3,1,128]{2,0,1:T(4,128)S(1)}, u32[]{:S(2)}, u32[]{:S(2)}) collective-permute-start(f32[3,1,128]{2,0,1:T(4,128)S(1)} %copy.79), channel_id=1, source_target_pairs={{0,4},{4,8},{8,12},{1,5},{5,9},{9,13},{2,6},{6,10},{10,14},{3,7},{... | collective-permute-start | bytes 4616 | tf_op jit(solution)/shard_map/ppermute | solution.py:16
  13.3 40.5 %collective-permute-start.3 = (f32[2,3,128]{2,1,0:T(4,128)S(1)}, f32[2,3,128]{2,1,0:T(4,128)S(1)}, u32[]{:S(2)}, u32[]{:S(2)}) collective-permute-start(f32[2,3,128]{2,1,0:T(4,128)S(1)} %pad_maximum_fusion.8), channel_id=1, source_target_pairs={{0,256},{16,272},{32,288},{48,304},{64,320},{80,336},{96,352},{112... | collective-permute-start | bytes 9224 | tf_op jit(solution)/shard_map/ppermute | solution.py:10
  18.8 34.8 %collective-permute-start.1 = (f32[3,32,1]{2,1,0:T(8,128)S(1)}, f32[3,32,1]{2,1,0:T(8,128)S(1)}, u32[]{:S(2)}, u32[]{:S(2)}) collective-permute-start(f32[3,32,1]{2,1,0:T(8,128)S(1)} %slice.98), channel_id=1, source_target_pairs={{0,16},{16,32},{32,48},{48,64},{64,80},{80,96},{96,112},{112,128},... | collective-permute-start | bytes 1160 | tf_op jit(solution)/shard_map/ppermute | solution.py:10
  28.4 8.7 %copy-start.2 = (f32[3,32,128]{2,1,0:T(8,128)S(1)}, f32[3,32,128]{2,1,0:T(8,128)}, u32[]{:S(2)}) copy-start(f32[3,32,128]{2,1,0:T(8,128)} %param.11) | copy-start | bytes 147460
  28.4 8.8 %copy-start.3 = (f32[3,32,128]{2,1,0:T(8,128)S(1)}, f32[3,32,128]{2,1,0:T(8,128)}, u32[]{:S(2)}) copy-start(f32[3,32,128]{2,1,0:T(8,128)} %param.14) | copy-start | bytes 147460
  28.4 8.8 %copy-start.1 = (f32[3,32,128]{2,1,0:T(8,128)S(1)}, f32[3,32,128]{2,1,0:T(8,128)}, u32[]{:S(2)}) copy-start(f32[3,32,128]{2,1,0:T(8,128)} %param.15) | copy-start | bytes 147460
  28.4 25.4 %copy-start.4 = (f32[3,32,128]{2,1,0:T(8,128)S(1)}, f32[3,32,128]{2,1,0:T(8,128)}, u32[]{:S(2)}) copy-start(f32[3,32,128]{2,1,0:T(8,128)} %param.12) | copy-start | bytes 147460
  28.4 27.6 %all-to-all-start = ((f32[128,2,4,4]{3,1,2,0:T(2,128)}), f32[128,2,4,4]{3,1,2,0:T(2,128)S(1)}, u32[]{:S(2)}, u32[]{:S(2)}) async-start(f32[128,2,4,4]{3,1,2,0:T(2,128)} %copy.40), calls=%async_computation | async-start | bytes 1048576 | tf_op jit(solution)/shard_map/all_to_all | solution.py:76
  37.1 79.8 %all-reduce.3.cloned.1.call-start = ((), (), s32[]{:S(2)}) async-start(), calls=%async_computation.1 | async-start | bytes 524288 | tf_op jit(solution)/shard_map/psum | solution.py:33
  37.2 24.0 %copy-start.7 = (pred[32]{0:T(512)(128)(4,1)}, pred[32]{0:T(512)(128)(4,1)S(1)}, u32[]{:S(2)}) copy-start(pred[32]{0:T(512)(128)(4,1)S(1)} %get-tuple-element.22) | copy-start | bytes 100
  37.2 103.3 %copy-start.5 = (pred[32]{0:T(512)(128)(4,1)}, pred[32]{0:T(512)(128)(4,1)S(1)}, u32[]{:S(2)}) copy-start(pred[32]{0:T(512)(128)(4,1)S(1)} %get-tuple-element.21) | copy-start | bytes 100
  56.4 4.8 %copy-start = (f32[12,3,32,128]{3,2,1,0:T(8,128)S(1)}, f32[12,3,32,128]{3,2,1,0:T(8,128)}, u32[]{:S(2)}) copy-start(f32[12,3,32,128]{3,2,1,0:T(8,128)} %param.10) | copy-start | bytes 1769476
  61.2 1.2 copy-start.9
  62.4 134.8 %all-reduce.5.cloned.1.call-start = ((), (), s32[]{:S(2)}) async-start(), calls=%async_computation.2 | async-start | bytes 524288 | tf_op jit(solution)/shard_map/psum | solution.py:33
  119.2 22.8 %collective-permute-start.4 = (f32[12,3,1,128]{3,0,2,1:T(8,128)}, f32[12,3,1,128]{3,0,2,1:T(8,128)}, u32[]{:S(2)}, u32[]{:S(2)}) collective-permute-start(f32[12,3,1,128]{3,0,2,1:T(8,128)} %get-tuple-element.14), channel_id=1, source_target_pairs={{0,256},{16,272},{32,288},{48,304},{64,320},{80,336},{96,352},{112... | collective-permute-start | bytes 55304 | tf_op jit(solution)/shard_map/ppermute | solution.py:10
  123.8 18.2 %collective-permute-start.7 = (f32[12,3,1,128]{3,0,2,1:T(8,128)}, f32[12,3,1,128]{3,0,2,1:T(8,128)}, u32[]{:S(2)}, u32[]{:S(2)}) collective-permute-start(f32[12,3,1,128]{3,0,2,1:T(8,128)} %get-tuple-element.15), channel_id=1, source_target_pairs={{0,4},{4,8},{8,12},{1,5},{5,9},{9,13},{2,6},{6,10},{10,14},{3,7},{... | collective-permute-start | bytes 55304 | tf_op jit(solution)/shard_map/ppermute | solution.py:26
  129.1 12.9 %collective-permute-start.5 = (f32[12,3,1,128]{3,0,2,1:T(8,128)}, f32[12,3,1,128]{3,0,2,1:T(8,128)}, u32[]{:S(2)}, u32[]{:S(2)}) collective-permute-start(f32[12,3,1,128]{3,0,2,1:T(8,128)} %get-tuple-element.16), channel_id=1, source_target_pairs={{4,0},{8,4},{12,8},{5,1},{9,5},{13,9},{6,2},{10,6},{14,10},{7,3},{... | collective-permute-start | bytes 55304 | tf_op jit(solution)/shard_map/ppermute | solution.py:27
  131.7 9.9 %collective-permute-start.2 = (f32[12,3,32,1]{2,3,1,0:T(1,128)S(1)}, f32[12,3,32,1]{2,3,1,0:T(1,128)S(1)}, u32[]{:S(2)}, u32[]{:S(2)}) collective-permute-start(f32[12,3,32,1]{2,3,1,0:T(1,128)S(1)} %copy.45), channel_id=1, source_target_pairs={{0,16},{16,32},{32,48},{48,64},{64,80},{80,96},{96,112},{112,128},... | collective-permute-start | bytes 13832 | tf_op jit(solution)/shard_map/ppermute | solution.py:26
  134.8 6.4 %collective-permute-start = (f32[12,3,32,1]{2,3,1,0:T(1,128)S(1)}, f32[12,3,32,1]{2,3,1,0:T(1,128)S(1)}, u32[]{:S(2)}, u32[]{:S(2)}) collective-permute-start(f32[12,3,32,1]{2,3,1,0:T(1,128)S(1)} %copy.43), channel_id=1, source_target_pairs={{16,0},{32,16},{48,32},{64,48},{80,64},{96,80},{112,96},{128,112},... | collective-permute-start | bytes 13832 | tf_op jit(solution)/shard_map/ppermute | solution.py:27
  198.4 26.1 %collective-permute-start.10 = (f32[12,3,1,128]{3,0,2,1:T(8,128)S(1)}, f32[12,3,1,128]{3,0,2,1:T(8,128)S(1)}, u32[]{:S(2)}, u32[]{:S(2)}) collective-permute-start(f32[12,3,1,128]{3,0,2,1:T(8,128)S(1)} %get-tuple-element.7), channel_id=1, source_target_pairs={{0,256},{16,272},{32,288},{48,304},{64,320},{80,336},{96,352},{112... | collective-permute-start | bytes 55304 | tf_op jit(solution)/shard_map/ppermute | solution.py:10
  202.9 21.5 %collective-permute-start.12 = (f32[12,3,1,128]{3,0,2,1:T(8,128)S(1)}, f32[12,3,1,128]{3,0,2,1:T(8,128)S(1)}, u32[]{:S(2)}, u32[]{:S(2)}) collective-permute-start(f32[12,3,1,128]{3,0,2,1:T(8,128)S(1)} %get-tuple-element.8), channel_id=1, source_target_pairs={{0,4},{4,8},{8,12},{1,5},{5,9},{9,13},{2,6},{6,10},{10,14},{3,7},{... | collective-permute-start | bytes 55304 | tf_op jit(solution)/shard_map/ppermute | solution.py:26
  208.2 16.2 %collective-permute-start.11 = (f32[12,3,1,128]{3,0,2,1:T(8,128)S(1)}, f32[12,3,1,128]{3,0,2,1:T(8,128)S(1)}, u32[]{:S(2)}, u32[]{:S(2)}) collective-permute-start(f32[12,3,1,128]{3,0,2,1:T(8,128)S(1)} %get-tuple-element.9), channel_id=1, source_target_pairs={{4,0},{8,4},{12,8},{5,1},{9,5},{13,9},{6,2},{10,6},{14,10},{7,3},{... | collective-permute-start | bytes 55304 | tf_op jit(solution)/shard_map/ppermute | solution.py:27
  210.8 7.3 %collective-permute-start.8 = (f32[12,3,32,1]{2,3,1,0:T(1,128)S(1)}, f32[12,3,32,1]{2,3,1,0:T(1,128)S(1)}, u32[]{:S(2)}, u32[]{:S(2)}) collective-permute-start(f32[12,3,32,1]{2,3,1,0:T(1,128)S(1)} %copy.49), channel_id=1, source_target_pairs={{16,0},{32,16},{48,32},{64,48},{80,64},{96,80},{112,96},{128,112},... | collective-permute-start | bytes 13832 | tf_op jit(solution)/shard_map/ppermute | solution.py:27
  216.2 8.3 %copy-start.6 = (pred[32]{0:T(512)(128)(4,1)S(1)}, pred[32]{0:T(512)(128)(4,1)}, u32[]{:S(2)}) copy-start(pred[32]{0:T(512)(128)(4,1)} %copy-done.5) | copy-start | bytes 100
  216.2 8.3 %copy-start.8 = (pred[32]{0:T(512)(128)(4,1)S(1)}, pred[32]{0:T(512)(128)(4,1)}, u32[]{:S(2)}) copy-start(pred[32]{0:T(512)(128)(4,1)} %copy-done.7) | copy-start | bytes 100
  216.2 7.8 %collective-permute-start.9 = (f32[12,3,32,1]{2,3,1,0:T(1,128)S(1)}, f32[12,3,32,1]{2,3,1,0:T(1,128)S(1)}, u32[]{:S(2)}, u32[]{:S(2)}) collective-permute-start(f32[12,3,32,1]{2,3,1,0:T(1,128)S(1)} %copy.51), channel_id=1, source_target_pairs={{0,16},{16,32},{32,48},{48,64},{64,80},{80,96},{96,112},{112,128},... | collective-permute-start | bytes 13832 | tf_op jit(solution)/shard_map/ppermute | solution.py:26
Sparse Core Ops, SparseCore 0:
  62.5 54.2 all-reduce.2
  144.6 52.6 all-reduce.4
